TPU v7x, 128 devices: a whole 4x4x4 slice. The times are simulated.
128 devices in a mesh: seq: 64 (over y, z, x), dp: 2 (over core).
Axes of the slice: x: 4, y: 4, z: 4, core: 2. Of those that a mesh axis runs over, the one named last changes fastest.
Arguments:
- queries: bfloat16 [131072, 768], P(('dp', 'seq')), parts along dimension 0, may hold values from -2.5 to 2.5
- keys: bfloat16 [131072, 768], P(('dp', 'seq')), parts along dimension 0, may hold values from -2.5 to 2.5
- values: bfloat16 [131072, 768], P(('dp', 'seq')), parts along dimension 0, may hold values from -6 to 6
- norm_gain: float32 [768], replicated, may hold values from 0.5 to 1.5
- expert_ids: int32 [131072, 1], P(('dp', 'seq')), parts along dimension 0, may hold values from 0 to 127; in each aligned block of 1024 rows (0 to 1023, 1024 to 2047, ...) at most 12 rows name the same one
- w_in: bfloat16 [256, 768, 3072], P(('dp', 'seq')), parts along dimension 0, may hold values from -0.21875 to 0.21875
- w_out: bfloat16 [256, 3072, 768], P(('dp', 'seq')), parts along dimension 0, may hold values from -0.109375 to 0.109375
Outputs:
- block_output: bfloat16 [131072, 768], P(('dp', 'seq')), parts along dimension 0
There are 2 independent parts, one for each index of `dp`. A program takes and returns all parts, laid end to end along the dimension named above; an argument that names none is the same for every part. Nothing has to cross between parts.
Inputs may be any that keep to these rules, and one draw needn't show every extreme that they name: `expert_ids`: within each aligned block of 1024 rows no expert is named more than 12 times, and in every draw some expert is named exactly 12 times in some block.
All inputs are finite; a program needn't handle non-finite values.
Results may differ from a plain program's by a relative error of at most 0.008.
Values may be sent and summed in bfloat16 or wider, within the bound.
A program may use at most 128 MiB of HBM per device.

v0:
```python
import jax
import jax.numpy as jnp
from jax import lax
from jax.sharding import PartitionSpec as P

HEADS = 12


epsilon = 1e-06


def shards(queries, keys, values, norm_gain, expert_ids, w_in, w_out):
    row_count = queries.shape[0]
    model_width = queries.shape[1]
    head_width = model_width // HEADS
    seq_count = lax.axis_size("seq")
    local_experts = w_in.shape[0]
    experts = local_experts * seq_count
    capacity = max(2, 3 * row_count // (2 * experts))
    query_heads = queries.reshape(row_count, HEADS, head_width)
    key_heads = keys.reshape(row_count, HEADS, head_width)
    value_heads = values.reshape(row_count, HEADS, head_width)
    block_state = jnp.einsum(
        "thd,the->hde", key_heads, value_heads, preferred_element_type=jnp.float32
    )
    block_state = block_state.reshape(HEADS, head_width * head_width)
    my_index = lax.axis_index("seq")
    piece = lax.all_gather(block_state[None], "seq", axis=0, tiled=True)
    keep = (jnp.arange(piece.shape[0], dtype=jnp.int32) < my_index).astype(jnp.float32)
    earlier = jnp.sum(piece * keep[:, None, None], axis=0)
    earlier = earlier.reshape(HEADS, head_width, head_width)
    scores = jnp.einsum("thd,shd->hts", query_heads, key_heads, preferred_element_type=jnp.float32)
    causal = jnp.arange(row_count)[:, None] >= jnp.arange(row_count)[None, :]
    scores = jnp.where(causal[None], scores, 0.0).astype(jnp.bfloat16)
    local_part = jnp.einsum("hts,shd->thd", scores, value_heads, preferred_element_type=jnp.float32)
    carried_part = jnp.einsum(
        "thd,hde->the", query_heads.astype(jnp.float32), earlier, precision=lax.Precision.HIGHEST
    )
    mixed = (local_part + carried_part).reshape(row_count, model_width)
    scale = lax.rsqrt(jnp.mean(mixed * mixed, axis=-1, keepdims=True) + epsilon)
    normed = (mixed * scale * norm_gain).astype(jnp.bfloat16)
    routes = expert_ids[:, 0]
    matches = (routes[:, None] == jnp.arange(experts, dtype=jnp.int32)[None, :]).astype(jnp.float32)
    lower_ones = causal.astype(jnp.float32)
    running = jnp.dot(lower_ones, matches, precision=lax.Precision.HIGHEST)
    slot_rank = (jnp.sum(running * matches, axis=1) - 1.0).astype(jnp.int32)
    slot_index = routes * capacity + slot_rank
    outgoing = jnp.zeros((experts * capacity, model_width), jnp.bfloat16).at[slot_index].set(normed)
    outgoing = outgoing.reshape(seq_count, local_experts, capacity, model_width)
    arrived = lax.all_to_all(outgoing, "seq", split_axis=0, concat_axis=0, tiled=True)
    hidden = jnp.einsum("secd,edf->secf", arrived, w_in, preferred_element_type=jnp.float32)
    hidden = jnp.maximum(hidden, 0.0).astype(jnp.bfloat16)
    finished = jnp.einsum(
        "secf,efd->secd", hidden, w_out, preferred_element_type=jnp.float32
    ).astype(jnp.bfloat16)
    returned = lax.all_to_all(finished, "seq", split_axis=0, concat_axis=0, tiled=True)
    expert_out = returned.reshape(experts * capacity, model_width)[slot_index]
    return (normed.astype(jnp.float32) + expert_out.astype(jnp.float32)).astype(jnp.bfloat16)


def solution(mesh):
    in_specs = (
        P(("dp", "seq"), None),
        P(("dp", "seq"), None),
        P(("dp", "seq"), None),
        P(),
        P(("dp", "seq"), None),
        P(("dp", "seq"), None, None),
        P(("dp", "seq"), None, None),
    )
    out_specs = P(("dp", "seq"), None)
    return jax.shard_map(shards, mesh=mesh, in_specs=in_specs, out_specs=out_specs, check_vma=False)
```

profile of v0, /device:TPU:0, one launch (start us, length us, event | category | flops | bytes accessed | tf_op | source)
XLA Modules:
  0.0 276.0 jit_solution(11601230091074444218)
XLA Ops:
  6.5 0.0 all-gather.2.cloned.1.call-start
  6.5 1.7 copy.28
  8.3 1.7 copy.29
  10.0 0.6 fusion.32
  10.5 0.0 copy-start.3
  10.6 0.8 broadcast_in_dim_reshape.3
  11.4 0.0 all-gather.2.cloned.1.call-update
  11.4 2.6 copy.27
  14.0 0.0 copy-done.3
  14.0 0.6 fusion.28
  14.6 1.3 iota_compare_fusion
  15.9 16.9 %fusion = f32[12,1024,64]{1,2,0:T(8,128)} fusion(bf16[1024,12,64]{0,2,1:T(8,128)(2,1)S(1)} %bitcast.47, pred[1024,1024]{1,0:T(8,128)(4,1)} %iota_compare_fusion, bf16[1024,12,64]{0,2,1:T(8,128)(2,1)} %bitcast.48, bf16[1024,12,64]{0,2,1:T(8,128)(2,1)S(1)} %bitcast.45), kind=kOutput, calls=%fused_computation.3 | convolution fusion | flops 3246391296 | bytes 8912896 | tf_op jit(solution)/shard_map/hts,shd->thd/dot_general | solution.py:35
  32.8 0.0 copy-start.1
  32.8 85.2 %all-gather.2.cloned.1.call-done = f32[64,12,4096]{2,1,0:T(8,128)} async-done(((f32[1,12,4096]{2,1,0:T(8,128)}), f32[64,12,4096]{2,1,0:T(8,128)}) %all-gather.2.cloned.1.call-update) | async-done | bytes 12582928 | tf_op jit(solution)/shard_map/all_gather | solution.py:28
  118.0 7.9 %multiply_reduce_fusion = f32[12,4096]{1,0:T(8,128)S(1)} fusion(f32[64,12,4096]{2,1,0:T(8,128)} %all-gather.2.cloned.1.call-done, f32[64]{0:T(128)S(1)} %compare_convert_fusion), kind=kLoop, calls=%fused_computation.8 | loop fusion | flops 6242304 | bytes 12779776 | tf_op jit(solution)/shard_map/reduce_sum | solution.py:30
  125.9 0.2 reshape.63
  126.0 0.0 copy-done.1
  126.1 5.2 %multiply_reduce_fusion.1 = (f32[1024]{0:T(1024)S(1)}, f32[1024,12,64]{0,2,1:T(8,128)}) fusion(f32[12,64,64]{2,1,0:T(8,128)S(1)} %reshape.63, bf16[1024,12,64]{0,2,1:T(8,128)(2,1)S(1)} %bitcast.49, f32[12,1024,64]{1,2,0:T(8,128)} %fusion), kind=kOutput, calls=%fused_computation.19 | convolution fusion | flops 606338048 | bytes 8065024 | tf_op jit(solution)/shard_map/thd,hde->the/dot_general | solution.py:36
  131.2 0.0 copy-start.2
  131.2 2.4 copy.31
  133.6 0.0 copy-start
  133.6 0.0 copy-done.2
  133.6 7.3 %scatter_custom_fusion = bf16[1536,768]{1,0:T(8,128)(2,1)} fusion(s32[1024]{0:T(1024)S(1)} %bitcast.50, bf16[]{:T(256)} %constant.9.clone.1, f32[1024,768]{1,0:T(8,128)S(1)} %copy.31, f32[768]{0:T(1024)S(1)} %copy-done.2, f32[1024]{0:T(1024)S(1)} %add_rsqrt_fusion), kind=kCustom, calls=%fused_computation.23 | custom fusion | flops 2359296 | bytes 5513218 | tf_op jit(solution)/shard_map/scatter | solution.py:48
  141.0 0.0 copy-done
  141.0 4.9 %reshape.65 = bf16[64,2,12,768]{3,2,1,0:T(8,128)(2,1)} reshape(bf16[1536,768]{1,0:T(8,128)(2,1)} %scatter_custom_fusion) | data formatting | bytes 4718592 | tf_op jit(solution)/shard_map/reshape | solution.py:49
  145.9 3.7 %copy.32 = bf16[64,2,12,768]{3,1,2,0:T(2,128)(2,1)S(1)} copy(bf16[64,2,12,768]{3,2,1,0:T(8,128)(2,1)} %reshape.65) | data formatting | bytes 4718592 | tf_op jit(solution)/shard_map/reshape | solution.py:49
  149.6 41.3 %all_to_all.10 = bf16[64,2,12,768]{3,1,2,0:T(2,128)(2,1)S(1)} all-to-all(bf16[64,2,12,768]{3,1,2,0:T(2,128)(2,1)S(1)} %copy.32), channel_id=1, replica_groups=mesh['seq'=64,'dp'=2] {'seq'}, dimensions={0} | all-to-all | bytes 4718592 | tf_op jit(solution)/shard_map/all_to_all | solution.py:50
  190.9 20.0 %convert_bitcast_fusion = bf16[64,2,12,768]{3,0,2,1:T(8,128)(2,1)} fusion(bf16[2,3072,768]{2,1,0:T(8,128)(2,1)} %param.13, bf16[2,768,3072]{2,1,0:T(8,128)(2,1)} %param.12, bf16[64,2,12,768]{3,1,2,0:T(2,128)(2,1)S(1)} %all_to_all.10), kind=kOutput, calls=%fused_computation.21 | convolution fusion | flops 14506131456 | bytes 23592960 | tf_op jit(solution)/shard_map/secf,efd->secd/dot_general | solution.py:53
  210.9 5.5 %copy.34 = bf16[64,2,12,768]{3,1,2,0:T(2,128)(2,1)} copy(bf16[64,2,12,768]{3,0,2,1:T(8,128)(2,1)} %convert_bitcast_fusion) | data formatting | bytes 4718592 | tf_op jit(solution)/shard_map/convert_element_type | solution.py:55
  216.4 4.9 %all-to-all-start.1 = ((bf16[64,2,12,768]{3,1,2,0:T(2,128)(2,1)}), bf16[64,2,12,768]{3,1,2,0:T(2,128)(2,1)S(1)}, u32[]{:S(2)}, u32[]{:S(2)}) async-start(bf16[64,2,12,768]{3,1,2,0:T(2,128)(2,1)} %copy.34), calls=%async_computation.1 | async-start | bytes 4718592 | tf_op jit(solution)/shard_map/all_to_all | solution.py:56
  221.3 32.6 %all-to-all-done.1 = bf16[64,2,12,768]{3,1,2,0:T(2,128)(2,1)S(1)} async-done(((bf16[64,2,12,768]{3,1,2,0:T(2,128)(2,1)}), bf16[64,2,12,768]{3,1,2,0:T(2,128)(2,1)S(1)}, u32[]{:S(2)}, u32[]{:S(2)}) %all-to-all-start.1) | async-done | bytes 2359328 | tf_op jit(solution)/shard_map/all_to_all | solution.py:56
  253.9 2.4 copy.35
  256.2 3.6 %reshape.66 = bf16[1536,768]{1,0:T(8,128)(2,1)S(1)} reshape(bf16[64,2,12,768]{3,2,1,0:T(8,128)(2,1)} %copy.35) | data formatting | bytes 4718592 | tf_op jit(solution)/shard_map/reshape | solution.py:57
  259.9 5.2 %gather_fusion = bf16[1024,768]{1,0:T(8,128)(2,1)} fusion(bf16[1536,768]{1,0:T(8,128)(2,1)S(1)} %reshape.66, s32[1024]{0:T(1024)S(1)} %broadcast_clamp_fusion), kind=kCustom, calls=%fused_computation | custom fusion | bytes 3149824 | tf_op jit(solution)/shard_map/gather | solution.py:57
  265.1 4.0 %add_convert_fusion = bf16[1024,768]{1,0:T(8,128)(2,1)} fusion(bf16[1024,768]{1,0:T(8,128)(2,1)} %gather_fusion, f32[768]{0:T(1024)S(1)} %copy-done.2, f32[1024,768]{1,0:T(8,128)} %copy-done, f32[1024]{0:T(1024)S(1)} %add_rsqrt_fusion), kind=kLoop, calls=%fused_computation.17 | loop fusion | flops 5505024 | bytes 6298624 | tf_op jit(solution)/shard_map/convert_element_type | solution.py:58
  (5 shorter events, 0.0 us)
Async XLA Ops:
  6.5 111.5 %all-gather.2.cloned.1.call-start = ((), (), s32[]{:S(2)}) async-start(), calls=%async_computation.2 | async-start | bytes 17039360 | tf_op jit(solution)/shard_map/all_gather | solution.py:28
  10.5 3.5 %copy-start.3 = (s32[1024,1]{0,1:T(1,128)S(1)}, s32[1024,1]{0,1:T(1,128)}, u32[]{:S(2)}) copy-start(s32[1024,1]{0,1:T(1,128)} %param.11) | copy-start | bytes 12292
  32.8 93.2 %copy-start.1 = (bf16[1024,768]{0,1:T(8,128)(2,1)S(1)}, bf16[1024,768]{0,1:T(8,128)(2,1)}, u32[]{:S(2)}) copy-start(bf16[1024,768]{0,1:T(8,128)(2,1)} %copy.27) | copy-start | bytes 4718596
  131.2 2.4 copy-start.2
  133.6 7.4 %copy-start = (f32[1024,768]{1,0:T(8,128)}, f32[1024,768]{1,0:T(8,128)S(1)}, u32[]{:S(2)}) copy-start(f32[1024,768]{1,0:T(8,128)S(1)} %copy.31) | copy-start | bytes 9437188
  216.4 37.5 %all-to-all-start.1 = ((bf16[64,2,12,768]{3,1,2,0:T(2,128)(2,1)}), bf16[64,2,12,768]{3,1,2,0:T(2,128)(2,1)S(1)}, u32[]{:S(2)}, u32[]{:S(2)}) async-start(bf16[64,2,12,768]{3,1,2,0:T(2,128)(2,1)} %copy.34), calls=%async_computation.1 | async-start | bytes 4718592 | tf_op jit(solution)/shard_map/all_to_all | solution.py:56
Sparse Core Ops, SparseCore 0:
  11.5 106.4 all-gather.1
where the time goes:
time: 277 us; the launch traced here: 276 us
  waiting for transfers between devices  118 us (43%)
  matrix products  43.3 us (16%)
  blocking collectives  41.3 us (15%)
  local copies, waits for them, and re-layouts  34.7 us (13%)
  other arithmetic  20.6 us (7%)
  between operations  13.5 us (5%)
  starting transfers between devices  4.86 us (2%)
    all_gather x1, waiting for transfers between devices, shards(): piece = lax.all_gather(block_state[None], 'seq', axis=0, tiled=True)  85.2 us
    all_to_all x1, blocking collectives, shards(): lax.all_to_all(outgoing, 'seq', split_axis=0, concat_axis=0, tiled=True)  41.3 us
    all_to_all x1, waiting for transfers between devices, shards(): lax.all_to_all(finished, 'seq', split_axis=0, concat_axis=0, tiled=True)  32.6 us
    dot_general x1, matrix products, shards(): jnp.einsum('secf,efd->secd', hidden, w_out, preferred_element_type=jnp.fl...  20 us
    dot_general x1, matrix products, shards(): jnp.einsum('hts,shd->thd', scores, value_heads, preferred_element_type=jn...  16.9 us
    reshape x2, local copies, waits for them, and re-layouts, shards(): outgoing = outgoing.reshape(seq_count, local_experts, capacity, model_width)  8.59 us
    reduce_sum x1, other arithmetic, shards(): earlier = jnp.sum(piece * keep[:, None, None], axis=0)  7.86 us
    scatter x1, other arithmetic, shards(): jnp.zeros((experts * capacity, model_width), jnp.bfloat16).at[slot_index]  7.34 us
  transfers between devices with their start and end apart: 2, of which 2 were waited for; matrix products, arithmetic and copies ran while one was open for 8% of the time, Pallas kernels for 0%

commit v1 on v0

v1 whole, which is shorter than its diff:
```python
import jax
import jax.numpy as jnp
from jax import lax
from jax.experimental import pallas as pl
from jax.experimental.pallas import tpu as pltpu
from jax.sharding import PartitionSpec as P

MESH = pl.DeviceIdType.MESH
EPS = 1e-06
F32 = jnp.float32
BF16 = jnp.bfloat16

N = 64
T = 1024
D = 768
FF = 3072
E = 128
PAIRS = 6
C = 256
NC = T // C
OWN = 48
CH = 3
M = 512


def dot(a, b):
    return jnp.dot(a, b, preferred_element_type=F32)


def dot_nt(a, b):
    return lax.dot_general(a, b, (((1,), (1,)), ((), ())), preferred_element_type=F32)


def dot_tn(a, b):
    return lax.dot_general(a, b, (((0,), (0,)), ((), ())), preferred_element_type=F32)


def lanes(p, width=128):
    return pl.ds(pl.multiple_of(p * width, width), width)


def body(q_hbm, k_hbm, v_hbm, gain_ref, ids_ref, win_hbm, wout_hbm, out_ref,
         q_ref, k_ref, v_ref, win, wout, kv_ref, cst_ref, mixed_ref, normed_ref,
         st_send, st_recv, pre_send, pre_recv, slot_ref, disp_send, disp_recv, ret_send, ret_recv,
         a_ref, h_ref, acc_ref,
         ld_sem, w_sem, self_sem, st_sem, pre_sem, disp_ssem, disp_rsem, ret_ssem, ret_rsem):
    me = lax.axis_index("seq")

    def remote(src, dst, ssem, rsem, d):
        return pltpu.make_async_remote_copy(
            src_ref=src, dst_ref=dst, send_sem=ssem, recv_sem=rsem,
            device_id={"seq": d}, device_id_type=MESH)

    barrier = pltpu.get_barrier_semaphore()

    def greet(o, _):
        pl.semaphore_signal(barrier, inc=1, device_id={"seq": lax.rem(me + o, N)}, device_id_type=MESH)
        return 0
    lax.fori_loop(1, N, greet, 0)

    loads = [pltpu.make_async_copy(s, d, ld_sem.at[i])
             for i, (s, d) in enumerate(((k_hbm, k_ref), (v_hbm, v_ref), (q_hbm, q_ref)))]
    for c in loads:
        c.start()
    weights = [pltpu.make_async_copy(s.at[e], d.at[e], w_sem.at[2 * e + i])
               for e in range(2) for i, (s, d) in enumerate(((win_hbm, win), (wout_hbm, wout)))]
    for c in weights:
        c.start()

    lane = lax.broadcasted_iota(jnp.int32, (1, 128), 1)
    low = lane < 64

    loads[0].wait()
    loads[1].wait()
    row128 = lax.broadcasted_iota(jnp.int32, (128, 128), 0)
    lane128 = lax.broadcasted_iota(jnp.int32, (128, 128), 1)
    diag = (row128 < 64) == (lane128 < 64)

    def states(p, _):
        total = jnp.zeros((128, 128), F32)
        for c in range(NC):
            kv_ref[p, c] = total
            kc = k_ref[c * C:(c + 1) * C, lanes(p)]
            vc = v_ref[c * C:(c + 1) * C, lanes(p)]
            total = total + jnp.where(diag, dot_tn(kc, vc), 0.0)
        compact = jnp.where(low, total[:64], total[64:])
        st_send[pl.ds(p * 8, 8)] = compact.reshape(8, 8, 128).astype(BF16)
        return 0
    lax.fori_loop(0, PAIRS, states, 0)

    pl.semaphore_wait(barrier, N - 1)

    def send_state(d, _):
        @pl.when(d != me)
        def _():
            remote(st_send.at[d], st_recv.at[me], st_sem.at[0], st_sem.at[1], d).start()
        return 0
    lax.fori_loop(0, OWN, send_state, 0)

    @pl.when(me < OWN)
    def _():
        pltpu.make_async_copy(st_send.at[me], st_recv.at[me], self_sem.at[0]).start()

    loads[2].wait()
    tri = lax.broadcasted_iota(jnp.int32, (C, C), 0) >= lax.broadcasted_iota(jnp.int32, (C, C), 1)

    def local(p, _):
        for c in range(NC):
            rows = slice(c * C, (c + 1) * C)
            qc = q_ref[rows, lanes(p)]
            kc = k_ref[rows, lanes(p)]
            vc = v_ref[rows, lanes(p)]
            zero = jnp.zeros_like(kc)
            s0 = jnp.where(tri, dot_nt(qc, jnp.where(low, kc, zero)), 0.0).astype(BF16)
            s1 = jnp.where(tri, dot_nt(qc, jnp.where(low, zero, kc)), 0.0).astype(BF16)
            mixed_ref[rows, lanes(p)] = dot(s0, jnp.where(low, vc, zero)) + dot(s1, jnp.where(low, zero, vc))
        return 0
    lax.fori_loop(0, 4, local, 0)

    @pl.when(me < OWN)
    def _():
        pltpu.make_async_copy(st_send.at[me], st_recv.at[me], self_sem.at[0]).wait()
        pltpu.make_async_copy(st_recv.at[pl.ds(0, N - 1)], st_recv.at[pl.ds(0, N - 1)], st_sem.at[1]).wait()

        def step(i, run):
            pre_send[i] = run.astype(BF16)
            return run + st_recv[i].astype(F32)
        lax.fori_loop(0, N, step, jnp.zeros((8, 128), F32), unroll=8)

        def send_prefix(o, _):
            d = lax.rem(me + o, N)
            remote(pre_send.at[d], pre_recv.at[me], pre_sem.at[0], pre_sem.at[1], d).start()
            return 0
        lax.fori_loop(1, N, send_prefix, 0)
        pltpu.make_async_copy(pre_send.at[me], pre_recv.at[me], self_sem.at[1]).start()

    lax.fori_loop(4, PAIRS, local, 0)

    ids = ids_ref[...]
    trib = jnp.where(lax.broadcasted_iota(jnp.int32, (C, C), 0) <= lax.broadcasted_iota(jnp.int32, (C, C), 1),
                     1.0, 0.0).astype(BF16)
    expert = lax.broadcasted_iota(jnp.int32, (E, C), 0)
    before = jnp.zeros((E, 1), F32)
    pieces = []
    for c in range(NC):
        idc = ids[:, c * C:(c + 1) * C]
        match = jnp.where(expert == idc, 1.0, 0.0)
        running = dot(match.astype(BF16), trib) + before
        rank = jnp.sum(running * match, axis=0, keepdims=True).astype(jnp.int32) - 1
        before = before + jnp.sum(match, axis=1, keepdims=True)
        half = lax.rem(idc, 2)
        owner = lax.div(idc, 2)
        pieces.append(jnp.where(rank < 8, half * M + owner * 8 + rank, 2 * M + owner * 8 + half * 4 + rank - 8))
    slot_row = jnp.concatenate(pieces, axis=1)
    slot_ref[...] = jnp.transpose(jnp.broadcast_to(slot_row.astype(F32), (128, T))).astype(jnp.int32)

    @pl.when(me < OWN)
    def _():
        pltpu.make_async_copy(pre_send.at[me], pre_recv.at[me], self_sem.at[1]).wait()
        pltpu.make_async_copy(pre_recv.at[pl.ds(0, OWN - 1)], pre_recv.at[pl.ds(0, OWN - 1)], pre_sem.at[1]).wait()

    @pl.when(me >= OWN)
    def _():
        pltpu.make_async_copy(pre_recv, pre_recv, pre_sem.at[1]).wait()

    for p in range(PAIRS):
        compact = pre_recv[pl.ds(p * 8, 8)].astype(F32).reshape(64, 128)
        cst_ref[p, :64] = jnp.where(low, compact, 0.0)
        cst_ref[p, 64:] = jnp.where(low, 0.0, compact)

    def finish(c, _):
        rows = pl.ds(pl.multiple_of(c * C, C), C)
        square = jnp.zeros((C, 128), F32)
        for p in range(PAIRS):
            cols = slice(p * 128, (p + 1) * 128)
            state = (kv_ref[p, c] + cst_ref[p]).astype(BF16)
            m = mixed_ref[rows, cols] + dot(q_ref[rows, cols], state)
            mixed_ref[rows, cols] = m
            square = square + m * m
        scale = lax.rsqrt(jnp.sum(square, axis=1, keepdims=True) * (1.0 / D) + EPS)
        normed_ref[rows, :] = (mixed_ref[rows, :] * scale * gain_ref[...]).astype(BF16)
        return 0
    lax.fori_loop(0, NC, finish, 0)

    for ch in range(CH):
        pick = jnp.where(lax.broadcasted_iota(jnp.int32, (M, T), 0) == slot_row - ch * M, 1.0, 0.0).astype(BF16)
        for n in range(3):
            y = dot(pick, normed_ref[:, n * 256:(n + 1) * 256])
            disp_send[ch, :, 2 * n] = y[:, :128].reshape(N, 8, 128).astype(BF16)
            disp_send[ch, :, 2 * n + 1] = y[:, 128:].reshape(N, 8, 128).astype(BF16)

        def send_rows(o, _):
            d = lax.rem(me + o * 21, N)
            remote(disp_send.at[ch, d], disp_recv.at[ch, me], disp_ssem.at[ch], disp_rsem.at[ch], d).start()
            return 0
        lax.fori_loop(1, N, send_rows, 0)
        pltpu.make_async_copy(disp_send.at[ch, me], disp_recv.at[ch, me], self_sem.at[2 + ch]).start()

    top = lax.broadcasted_iota(jnp.int32, (1, 8, 128), 1) < 4

    def ffn(e, start, rows, put):
        def first(f, _):
            hid = dot(a_ref[start:start + rows, :], win[e, :, lanes(f, 256)])
            h_ref[start:start + rows, lanes(f, 256)] = jnp.maximum(hid, 0.0).astype(BF16)
            return 0
        lax.fori_loop(0, FF // 256, first, 0)

        def second(n, _):
            put(n, dot(h_ref[start:start + rows, :], wout[e, :, lanes(n, 256)]))
            return 0
        lax.fori_loop(0, D // 256, second, 0)

    def bulk(buf, sem):
        return pltpu.make_async_copy(buf.at[pl.ds(0, N - 1)], buf.at[pl.ds(0, N - 1)], sem)

    for ch in range(CH):
        pltpu.make_async_copy(disp_send.at[ch, me], disp_recv.at[ch, me], self_sem.at[2 + ch]).wait()
        bulk(disp_recv.at[ch], disp_rsem.at[ch]).wait()
        if ch < 2:
            weights[2 * ch].wait()
            weights[2 * ch + 1].wait()
            for j in range(6):
                a_ref[:, j * 128:(j + 1) * 128] = disp_recv[ch, :, j].astype(F32).reshape(M, 128).astype(BF16)

            def put(n, o):
                ret_send[ch, :, 2 * n] = o[:, :128].reshape(N, 8, 128).astype(BF16)
                ret_send[ch, :, 2 * n + 1] = o[:, 128:].reshape(N, 8, 128).astype(BF16)
            ffn(ch, 0, M, put)
        else:
            for j in range(6):
                x = disp_recv[ch, :, j].astype(F32).reshape(N // 2, 2, 8, 128)
                even, odd = x[:, 0], x[:, 1]
                x0 = jnp.where(top, even, pltpu.roll(odd, 4, 1))
                x1 = jnp.where(top, pltpu.roll(even, 4, 1), odd)
                a_ref[:256, j * 128:(j + 1) * 128] = x0.reshape(256, 128).astype(BF16)
                a_ref[256:, j * 128:(j + 1) * 128] = x1.reshape(256, 128).astype(BF16)

            def put0(n, o):
                acc_ref[:256, lanes(n, 256)] = o

            def put1(n, o):
                acc_ref[256:512, lanes(n, 256)] = o
            ffn(0, 0, 256, put0)
            ffn(1, 256, 256, put1)
            for j in range(6):
                o0 = acc_ref[:256, j * 128:(j + 1) * 128].reshape(N // 2, 8, 128)
                o1 = acc_ref[256:512, j * 128:(j + 1) * 128].reshape(N // 2, 8, 128)
                even = jnp.where(top, o0, pltpu.roll(o1, 4, 1))
                odd = jnp.where(top, pltpu.roll(o0, 4, 1), o1)
                ret_send[ch, :, j] = jnp.stack([even, odd], axis=1).reshape(N, 8, 128).astype(BF16)

        def send_back(o, _):
            d = lax.rem(me + o * 21, N)
            remote(ret_send.at[ch, d], ret_recv.at[ch, me], ret_ssem.at[ch], ret_rsem.at[ch], d).start()
            return 0
        lax.fori_loop(1, N, send_back, 0)
        pltpu.make_async_copy(ret_send.at[ch, me], ret_recv.at[ch, me], self_sem.at[5 + ch]).start()

    for ch in range(CH):
        pltpu.make_async_copy(ret_send.at[ch, me], ret_recv.at[ch, me], self_sem.at[5 + ch]).wait()
        bulk(ret_recv.at[ch], ret_rsem.at[ch]).wait()
        for j in range(6):
            a_ref[:, j * 128:(j + 1) * 128] = ret_recv[ch, :, j].astype(F32).reshape(M, 128).astype(BF16)

        def unpack(c, _):
            rows = pl.ds(pl.multiple_of(c * C, C), C)
            place = slot_ref[rows, :] - ch * M
            back = jnp.concatenate([jnp.where(place == lane + 128 * i, 1.0, 0.0).astype(BF16) for i in range(M // 128)], axis=1)
            for n in range(3):
                cols = slice(n * 256, (n + 1) * 256)
                y = dot(back, a_ref[:, cols])
                if ch == 0:
                    acc_ref[rows, cols] = y
                elif ch == 1:
                    acc_ref[rows, cols] = acc_ref[rows, cols] + y
                else:
                    total = acc_ref[rows, cols] + y
                    out_ref[rows, cols] = (normed_ref[rows, cols].astype(F32) + total).astype(BF16)
            return 0
        lax.fori_loop(0, NC, unpack, 0)

    @pl.when(me < OWN)
    def _():
        pltpu.make_async_copy(st_send.at[pl.ds(0, OWN - 1)], st_send.at[pl.ds(0, OWN - 1)], st_sem.at[0]).wait()
        bulk(pre_send, pre_sem.at[0]).wait()

    @pl.when(me >= OWN)
    def _():
        pltpu.make_async_copy(st_send, st_send, st_sem.at[0]).wait()
    for ch in range(CH):
        bulk(disp_send.at[ch], disp_ssem.at[ch]).wait()
        bulk(ret_send.at[ch], ret_ssem.at[ch]).wait()


def shards(queries, keys, values, norm_gain, expert_ids, w_in, w_out):
    hbm = pl.BlockSpec(memory_space=pl.ANY)
    vmem = pl.BlockSpec(memory_space=pltpu.VMEM)
    dma = pltpu.SemaphoreType.DMA
    return pl.pallas_call(
        body,
        out_shape=jax.ShapeDtypeStruct((T, D), BF16),
        in_specs=[hbm, hbm, hbm, vmem, vmem, hbm, hbm],
        out_specs=vmem,
        scratch_shapes=[
            pltpu.VMEM((T, D), BF16), pltpu.VMEM((T, D), BF16), pltpu.VMEM((T, D), BF16),
            pltpu.VMEM((2, D, FF), BF16), pltpu.VMEM((2, FF, D), BF16),
            pltpu.VMEM((PAIRS, NC, 128, 128), F32), pltpu.VMEM((PAIRS, 128, 128), F32),
            pltpu.VMEM((T, D), F32), pltpu.VMEM((T, D), BF16),
            pltpu.VMEM((OWN, 8, 128), BF16), pltpu.VMEM((N, 8, 128), BF16),
            pltpu.VMEM((N, 8, 128), BF16), pltpu.VMEM((OWN, 8, 128), BF16),
            pltpu.VMEM((T, 128), jnp.int32),
            pltpu.VMEM((CH, N, 6, 8, 128), BF16), pltpu.VMEM((CH, N, 6, 8, 128), BF16),
            pltpu.VMEM((CH, N, 6, 8, 128), BF16), pltpu.VMEM((CH, N, 6, 8, 128), BF16),
            pltpu.VMEM((M, D), BF16), pltpu.VMEM((M, FF), BF16), pltpu.VMEM((T, D), F32),
            dma((3,)), dma((4,)), dma((8,)), dma((2,)), dma((2,)),
            dma((CH,)), dma((CH,)), dma((CH,)), dma((CH,)),
        ],
        compiler_params=pltpu.CompilerParams(
            collective_id=0, has_side_effects=True, vmem_limit_bytes=67043328),
        name="block",
    )(queries, keys, values, norm_gain.reshape(1, D), expert_ids.reshape(1, T), w_in, w_out)


def solution(mesh):
    rows = P(("dp", "seq"), None)
    weights = P(("dp", "seq"), None, None)
    return jax.shard_map(
        shards, mesh=mesh, in_specs=(rows, rows, rows, P(), rows, weights, weights),
        out_specs=rows, check_vma=False)
```

time: 277 us -> 91.3 us (0.33)
  waiting for transfers between devices: 118 us -> 0 us
  Pallas kernels: 0 us -> 86.8 us
  matrix products: 43.3 us -> 0 us
  blocking collectives: 41.3 us -> 0 us
  local copies, waits for them, and re-layouts: 34.7 us -> 3.92 us
  other arithmetic: 20.6 us -> 0 us
  between operations: 13.5 us -> 0.01 us
  starting transfers between devices: 4.86 us -> 0 us
    pallas_call x0 -> x1, Pallas kernels: none -> 86.8 us  [shards(): pl.pallas_call(body, out_shape=jax.ShapeDtypeStruct((T, D), BF16), in_spe...]
    all_gather x1 -> x0, waiting for transfers between devices: 85.2 us -> none  [shards(): piece = lax.all_gather(block_state[None], 'seq', axis=0, tiled=True)]
    dot_general x5 -> x0, matrix products: 43.3 us -> none  [the longest x1 20 us: shards(): jnp.einsum('secf,efd->secd', hidden, w_out, preferred_element_type=jnp.fl...]
    all_to_all x1 -> x0, blocking collectives: 41.3 us -> none  [shards(): lax.all_to_all(outgoing, 'seq', split_axis=0, concat_axis=0, tiled=True)]
    all_to_all x1 -> x0, waiting for transfers between devices: 32.6 us -> none  [shards(): lax.all_to_all(finished, 'seq', split_axis=0, concat_axis=0, tiled=True)]
    reshape x5 -> x1, local copies, waits for them, and re-layouts: 14.8 us -> 1.27 us  [shards(): norm_gain.reshape(1, D)]
    reduce_sum x1 -> x0, other arithmetic: 7.86 us -> none  [shards(): earlier = jnp.sum(piece * keep[:, None, None], axis=0)]
    scatter x1 -> x0, other arithmetic: 7.34 us -> none  [shards(): jnp.zeros((experts * capacity, model_width), jnp.bfloat16).at[slot_index]]
  transfers between devices with their start and end apart: 2 -> 0, of which waited for: 2 -> 0; matrix products, arithmetic and copies ran while one was open for 8% -> 0% of each run, Pallas kernels for 0% -> 0%
where the time goes in v1:
time: 91.3 us; the launch traced here: 90.7 us
  Pallas kernels  86.8 us (95%)
  local copies, waits for them, and re-layouts  3.92 us (4%)
    pallas_call x1, Pallas kernels, shards(): pl.pallas_call(body, out_shape=jax.ShapeDtypeStruct((T, D), BF16), in_spe...  86.8 us
    unnamed x1, local copies, waits for them, and re-layouts  2.65 us

profile of v1, /device:TPU:0, one launch (start us, length us, event | category | flops | bytes accessed | tf_op | source)
XLA Modules:
  0.0 90.7 jit_solution(12466873711912729219)
XLA Ops:
  0.0 1.3 %reshape.6.gain_ref = f32[1,768]{1,0:T(1,128)} reshape(f32[768]{0:T(1024)} %param.10) | data formatting | bytes 6144 | tf_op jit(solution)/shard_map/reshape | solution.py:321
  1.3 86.8 %block.1 = bf16[1024,768]{1,0:T(8,128)(2,1)} custom-call(bf16[1024,768]{1,0:T(8,128)(2,1)} %q_hbm.1, bf16[1024,768]{1,0:T(8,128)(2,1)} %k_hbm.1, bf16[1024,768]{1,0:T(8,128)(2,1)} %v_hbm.1, f32[1,768]{1,0:T(1,128)} %reshape.6.gain_ref, s32[1,1024]{1,0:T(1,128)} %bitcast.1, bf16[2,768,3072]{2,1,0:T(8,128)(2,1)} %win_hbm.1, bf16[2,3072,768]{2,1,0:T(8,128)(2,1)} %wout_hbm.1), custom_call_target="tpu_custom_call" | custom-call | tf_op jit(solution)/shard_map/block/pallas_call | solution.py:299
  88.0 2.7 %copy.9 = bf16[1024,768]{1,0:T(8,128)(2,1)} copy(bf16[1024,768]{1,0:T(8,128)(2,1)} %block.1) | data formatting | bytes 3145728

commit v2 on v1

--- a/solution.py
+++ b/solution.py
@@ -23,6 +23,14 @@
 M = 512
 
 
+def hops(o):
+    return sum((0, 1, 2, 1)[g] for g in (o // 16, o // 4 % 4, o % 4))
+
+
+ORDER = sorted(range(1, N), key=lambda o: (-hops(o), o * 37 % 64))
+MIXED = [o * 21 % 64 for o in range(1, N)]
+
+
 def dot(a, b):
     return jnp.dot(a, b, preferred_element_type=F32)
 
@@ -39,12 +47,25 @@
     return pl.ds(pl.multiple_of(p * width, width), width)
 
 
-def body(q_hbm, k_hbm, v_hbm, gain_ref, ids_ref, win_hbm, wout_hbm, out_ref,
-         q_ref, k_ref, v_ref, win, wout, kv_ref, cst_ref, mixed_ref, normed_ref,
-         st_send, st_recv, pre_send, pre_recv, slot_ref, disp_send, disp_recv, ret_send, ret_recv,
+def spread(place):
+    lane = lax.broadcasted_iota(jnp.int32, (1, 128), 1)
+    return jnp.concatenate([jnp.where(place == lane + 128 * i, 1.0, 0.0).astype(BF16) for i in range(M // 128)], axis=1)
+
+
+def body(q_hbm, k_hbm, v_hbm, gain_hbm, ids_hbm, win_hbm, wout_hbm,
+         out_ref,
+         gain_ref, ids_ref, q_ref, k_ref, v_ref, win, wout, kv_ref, cst_ref, mixed_ref, normed_ref,
+         st_send, st_recv, pre_send, pre_recv, slot_ref, early_ref, earlyq_ref, disp_send, disp_recv, ret_send, ret_recv,
          a_ref, h_ref, acc_ref,
          ld_sem, w_sem, self_sem, st_sem, pre_sem, disp_ssem, disp_rsem, ret_ssem, ret_rsem):
     me = lax.axis_index("seq")
+    my, mz, mx = me // 16, lax.rem(me // 4, 4), lax.rem(me, 4)
+    ys = [lax.rem(my + g, 4) * 16 for g in range(4)]
+    zs = [lax.rem(mz + g, 4) * 4 for g in range(4)]
+    xs = [lax.rem(mx + g, 4) for g in range(4)]
+
+    def other(o):
+        return ys[o // 16] + zs[o // 4 % 4] + xs[o % 4]
 
     def remote(src, dst, ssem, rsem, d):
         return pltpu.make_async_remote_copy(
@@ -53,13 +74,11 @@
 
     barrier = pltpu.get_barrier_semaphore()
 
-    def greet(o, _):
-        pl.semaphore_signal(barrier, inc=1, device_id={"seq": lax.rem(me + o, N)}, device_id_type=MESH)
-        return 0
-    lax.fori_loop(1, N, greet, 0)
+    for o in ORDER:
+        pl.semaphore_signal(barrier, inc=1, device_id={"seq": other(o)}, device_id_type=MESH)
 
     loads = [pltpu.make_async_copy(s, d, ld_sem.at[i])
-             for i, (s, d) in enumerate(((k_hbm, k_ref), (v_hbm, v_ref), (q_hbm, q_ref)))]
+             for i, (s, d) in enumerate(((k_hbm, k_ref), (v_hbm, v_ref), (ids_hbm, ids_ref), (gain_hbm, gain_ref), (q_hbm, q_ref)))]
     for c in loads:
         c.start()
     weights = [pltpu.make_async_copy(s.at[e], d.at[e], w_sem.at[2 * e + i])
@@ -88,54 +107,8 @@
         return 0
     lax.fori_loop(0, PAIRS, states, 0)
 
-    pl.semaphore_wait(barrier, N - 1)
-
-    def send_state(d, _):
-        @pl.when(d != me)
-        def _():
-            remote(st_send.at[d], st_recv.at[me], st_sem.at[0], st_sem.at[1], d).start()
-        return 0
-    lax.fori_loop(0, OWN, send_state, 0)
-
-    @pl.when(me < OWN)
-    def _():
-        pltpu.make_async_copy(st_send.at[me], st_recv.at[me], self_sem.at[0]).start()
-
     loads[2].wait()
-    tri = lax.broadcasted_iota(jnp.int32, (C, C), 0) >= lax.broadcasted_iota(jnp.int32, (C, C), 1)
-
-    def local(p, _):
-        for c in range(NC):
-            rows = slice(c * C, (c + 1) * C)
-            qc = q_ref[rows, lanes(p)]
-            kc = k_ref[rows, lanes(p)]
-            vc = v_ref[rows, lanes(p)]
-            zero = jnp.zeros_like(kc)
-            s0 = jnp.where(tri, dot_nt(qc, jnp.where(low, kc, zero)), 0.0).astype(BF16)
-            s1 = jnp.where(tri, dot_nt(qc, jnp.where(low, zero, kc)), 0.0).astype(BF16)
-            mixed_ref[rows, lanes(p)] = dot(s0, jnp.where(low, vc, zero)) + dot(s1, jnp.where(low, zero, vc))
-        return 0
-    lax.fori_loop(0, 4, local, 0)
-
-    @pl.when(me < OWN)
-    def _():
-        pltpu.make_async_copy(st_send.at[me], st_recv.at[me], self_sem.at[0]).wait()
-        pltpu.make_async_copy(st_recv.at[pl.ds(0, N - 1)], st_recv.at[pl.ds(0, N - 1)], st_sem.at[1]).wait()
-
-        def step(i, run):
-            pre_send[i] = run.astype(BF16)
-            return run + st_recv[i].astype(F32)
-        lax.fori_loop(0, N, step, jnp.zeros((8, 128), F32), unroll=8)
-
-        def send_prefix(o, _):
-            d = lax.rem(me + o, N)
-            remote(pre_send.at[d], pre_recv.at[me], pre_sem.at[0], pre_sem.at[1], d).start()
-            return 0
-        lax.fori_loop(1, N, send_prefix, 0)
-        pltpu.make_async_copy(pre_send.at[me], pre_recv.at[me], self_sem.at[1]).start()
-
-    lax.fori_loop(4, PAIRS, local, 0)
-
+    loads[3].wait()
     ids = ids_ref[...]
     trib = jnp.where(lax.broadcasted_iota(jnp.int32, (C, C), 0) <= lax.broadcasted_iota(jnp.int32, (C, C), 1),
                      1.0, 0.0).astype(BF16)
@@ -154,6 +127,61 @@
     slot_row = jnp.concatenate(pieces, axis=1)
     slot_ref[...] = jnp.transpose(jnp.broadcast_to(slot_row.astype(F32), (128, T))).astype(jnp.int32)
 
+    pl.semaphore_wait(barrier, N - 1)
+    for o in ORDER:
+        d = other(o)
+
+        @pl.when(d < OWN)
+        def _(d=d):
+            remote(st_send.at[d], st_recv.at[me], st_sem.at[0], st_sem.at[1], d).start()
+
+    @pl.when(me < OWN)
+    def _():
+        pltpu.make_async_copy(st_send.at[me], st_recv.at[me], self_sem.at[0]).start()
+
+    loads[4].wait()
+    tri = lax.broadcasted_iota(jnp.int32, (C, C), 0) >= lax.broadcasted_iota(jnp.int32, (C, C), 1)
+
+    def local(p, _):
+        for c in range(NC):
+            rows = slice(c * C, (c + 1) * C)
+            qc = q_ref[rows, lanes(p)]
+            kc = k_ref[rows, lanes(p)]
+            vc = v_ref[rows, lanes(p)]
+            zero = jnp.zeros_like(kc)
+            s0 = jnp.where(tri, dot_nt(qc, jnp.where(low, kc, zero)), 0.0).astype(BF16)
+            s1 = jnp.where(tri, dot_nt(qc, jnp.where(low, zero, kc)), 0.0).astype(BF16)
+            mixed_ref[rows, lanes(p)] = (dot(s0, jnp.where(low, vc, zero)) + dot(s1, jnp.where(low, zero, vc))
+                                         + dot(qc, kv_ref[p, c].astype(BF16)))
+        return 0
+    lax.fori_loop(0, PAIRS, local, 0)
+
+    @pl.when(me < OWN)
+    def _():
+        pltpu.make_async_copy(st_send.at[me], st_recv.at[me], self_sem.at[0]).wait()
+        pltpu.make_async_copy(st_recv.at[pl.ds(0, N - 1)], st_recv.at[pl.ds(0, N - 1)], st_sem.at[1]).wait()
+
+        def step(i, run):
+            pre_send[i] = run.astype(BF16)
+            return run + st_recv[i].astype(F32)
+        lax.fori_loop(0, N, step, jnp.zeros((8, 128), F32), unroll=8)
+
+        for o in ORDER:
+            d = other(o)
+            remote(pre_send.at[d], pre_recv.at[me], pre_sem.at[0], pre_sem.at[1], d).start()
+        pltpu.make_async_copy(pre_send.at[me], pre_recv.at[me], self_sem.at[1]).start()
+
+    def pick(ch):
+        return jnp.where(lax.broadcasted_iota(jnp.int32, (M, T), 0) == slot_row - ch * M, 1.0, 0.0).astype(BF16)
+
+    first_pick = pick(0)
+    for n in range(3):
+        cols = slice(n * 256, (n + 1) * 256)
+        m = mixed_ref[:, cols]
+        high = m.astype(BF16)
+        early_ref[:, cols] = dot(first_pick, high) + dot(first_pick, (m - high.astype(F32)).astype(BF16))
+        earlyq_ref[:, cols] = dot(first_pick, q_ref[:, cols]).astype(BF16)
+
     @pl.when(me < OWN)
     def _():
         pltpu.make_async_copy(pre_send.at[me], pre_recv.at[me], self_sem.at[1]).wait()
@@ -165,36 +193,54 @@
 
     for p in range(PAIRS):
         compact = pre_recv[pl.ds(p * 8, 8)].astype(F32).reshape(64, 128)
-        cst_ref[p, :64] = jnp.where(low, compact, 0.0)
-        cst_ref[p, 64:] = jnp.where(low, 0.0, compact)
+        cst_ref[p, :64] = jnp.where(low, compact, 0.0).astype(BF16)
+        cst_ref[p, 64:] = jnp.where(low, 0.0, compact).astype(BF16)
+
+    gain = gain_ref[...].reshape(1, D)
+
+    def send_rows(ch):
+        for o in MIXED:
+            d = other(o)
+            remote(disp_send.at[ch, d], disp_recv.at[ch, me], disp_ssem.at[ch], disp_rsem.at[ch], d).start()
+        pltpu.make_async_copy(disp_send.at[ch, me], disp_recv.at[ch, me], self_sem.at[2 + ch]).start()
+
+    def finish_early(c, _):
+        rows = pl.ds(pl.multiple_of(c * 128, 128), 128)
+        square = jnp.zeros((128, 128), F32)
+        ms = []
+        for p in range(PAIRS):
+            cols = slice(p * 128, (p + 1) * 128)
+            m = early_ref[rows, cols] + dot(earlyq_ref[rows, cols], cst_ref[p])
+            ms.append(m)
+            square = square + m * m
+        scale = lax.rsqrt(jnp.sum(square, axis=1, keepdims=True) * (1.0 / D) + EPS)
+        for p in range(PAIRS):
+            y = ms[p] * scale * gain[:, p * 128:(p + 1) * 128]
+            disp_send[0, pl.ds(c * 16, 16), p] = y.reshape(16, 8, 128).astype(BF16)
+        return 0
+    lax.fori_loop(0, M // 128, finish_early, 0)
+    send_rows(0)
 
     def finish(c, _):
         rows = pl.ds(pl.multiple_of(c * C, C), C)
         square = jnp.zeros((C, 128), F32)
         for p in range(PAIRS):
             cols = slice(p * 128, (p + 1) * 128)
-            state = (kv_ref[p, c] + cst_ref[p]).astype(BF16)
-            m = mixed_ref[rows, cols] + dot(q_ref[rows, cols], state)
+            m = mixed_ref[rows, cols] + dot(q_ref[rows, cols], cst_ref[p])
             mixed_ref[rows, cols] = m
             square = square + m * m
         scale = lax.rsqrt(jnp.sum(square, axis=1, keepdims=True) * (1.0 / D) + EPS)
-        normed_ref[rows, :] = (mixed_ref[rows, :] * scale * gain_ref[...]).astype(BF16)
+        normed_ref[rows, :] = (mixed_ref[rows, :] * scale * gain).astype(BF16)
         return 0
     lax.fori_loop(0, NC, finish, 0)
 
-    for ch in range(CH):
-        pick = jnp.where(lax.broadcasted_iota(jnp.int32, (M, T), 0) == slot_row - ch * M, 1.0, 0.0).astype(BF16)
+    for ch in range(1, CH):
+        this_pick = pick(ch)
         for n in range(3):
-            y = dot(pick, normed_ref[:, n * 256:(n + 1) * 256])
+            y = dot(this_pick, normed_ref[:, n * 256:(n + 1) * 256])
             disp_send[ch, :, 2 * n] = y[:, :128].reshape(N, 8, 128).astype(BF16)
             disp_send[ch, :, 2 * n + 1] = y[:, 128:].reshape(N, 8, 128).astype(BF16)
-
-        def send_rows(o, _):
-            d = lax.rem(me + o * 21, N)
-            remote(disp_send.at[ch, d], disp_recv.at[ch, me], disp_ssem.at[ch], disp_rsem.at[ch], d).start()
-            return 0
-        lax.fori_loop(1, N, send_rows, 0)
-        pltpu.make_async_copy(disp_send.at[ch, me], disp_recv.at[ch, me], self_sem.at[2 + ch]).start()
+        send_rows(ch)
 
     top = lax.broadcasted_iota(jnp.int32, (1, 8, 128), 1) < 4
 
@@ -249,11 +295,9 @@
                 odd = jnp.where(top, pltpu.roll(o0, 4, 1), o1)
                 ret_send[ch, :, j] = jnp.stack([even, odd], axis=1).reshape(N, 8, 128).astype(BF16)
 
-        def send_back(o, _):
-            d = lax.rem(me + o * 21, N)
+        for o in (MIXED if ch < 2 else ORDER):
+            d = other(o)
             remote(ret_send.at[ch, d], ret_recv.at[ch, me], ret_ssem.at[ch], ret_rsem.at[ch], d).start()
-            return 0
-        lax.fori_loop(1, N, send_back, 0)
         pltpu.make_async_copy(ret_send.at[ch, me], ret_recv.at[ch, me], self_sem.at[5 + ch]).start()
 
     for ch in range(CH):
@@ -264,18 +308,16 @@
 
         def unpack(c, _):
             rows = pl.ds(pl.multiple_of(c * C, C), C)
-            place = slot_ref[rows, :] - ch * M
-            back = jnp.concatenate([jnp.where(place == lane + 128 * i, 1.0, 0.0).astype(BF16) for i in range(M // 128)], axis=1)
+            back = spread(slot_ref[rows, :] - ch * M)
             for n in range(3):
                 cols = slice(n * 256, (n + 1) * 256)
                 y = dot(back, a_ref[:, cols])
                 if ch == 0:
                     acc_ref[rows, cols] = y
                 elif ch == 1:
-                    acc_ref[rows, cols] = acc_ref[rows, cols] + y
+                    acc_ref[rows, cols] = normed_ref[rows, cols].astype(F32) + (acc_ref[rows, cols] + y)
                 else:
-                    total = acc_ref[rows, cols] + y
-                    out_ref[rows, cols] = (normed_ref[rows, cols].astype(F32) + total).astype(BF16)
+                    out_ref[rows, cols] = (acc_ref[rows, cols] + y).astype(BF16)
             return 0
         lax.fori_loop(0, NC, unpack, 0)
 
@@ -293,32 +335,34 @@
 
 
 def shards(queries, keys, values, norm_gain, expert_ids, w_in, w_out):
-    hbm = pl.BlockSpec(memory_space=pl.ANY)
+    hbm = pl.BlockSpec(memory_space=pltpu.HBM)
     vmem = pl.BlockSpec(memory_space=pltpu.VMEM)
     dma = pltpu.SemaphoreType.DMA
     return pl.pallas_call(
         body,
         out_shape=jax.ShapeDtypeStruct((T, D), BF16),
-        in_specs=[hbm, hbm, hbm, vmem, vmem, hbm, hbm],
+        in_specs=[hbm] * 7,
         out_specs=vmem,
         scratch_shapes=[
+            pltpu.VMEM((D,), F32), pltpu.VMEM((1, T), jnp.int32),
             pltpu.VMEM((T, D), BF16), pltpu.VMEM((T, D), BF16), pltpu.VMEM((T, D), BF16),
             pltpu.VMEM((2, D, FF), BF16), pltpu.VMEM((2, FF, D), BF16),
-            pltpu.VMEM((PAIRS, NC, 128, 128), F32), pltpu.VMEM((PAIRS, 128, 128), F32),
+            pltpu.VMEM((PAIRS, NC, 128, 128), F32), pltpu.VMEM((PAIRS, 128, 128), BF16),
             pltpu.VMEM((T, D), F32), pltpu.VMEM((T, D), BF16),
             pltpu.VMEM((OWN, 8, 128), BF16), pltpu.VMEM((N, 8, 128), BF16),
             pltpu.VMEM((N, 8, 128), BF16), pltpu.VMEM((OWN, 8, 128), BF16),
-            pltpu.VMEM((T, 128), jnp.int32),
+            pltpu.VMEM((T, 128), jnp.int32), pltpu.VMEM((M, D), F32), pltpu.VMEM((M, D), BF16),
             pltpu.VMEM((CH, N, 6, 8, 128), BF16), pltpu.VMEM((CH, N, 6, 8, 128), BF16),
             pltpu.VMEM((CH, N, 6, 8, 128), BF16), pltpu.VMEM((CH, N, 6, 8, 128), BF16),
             pltpu.VMEM((M, D), BF16), pltpu.VMEM((M, FF), BF16), pltpu.VMEM((T, D), F32),
-            dma((3,)), dma((4,)), dma((8,)), dma((2,)), dma((2,)),
+            dma((5,)), dma((4,)), dma((8,)), dma((2,)), dma((2,)),
             dma((CH,)), dma((CH,)), dma((CH,)), dma((CH,)),
         ],
         compiler_params=pltpu.CompilerParams(
-            collective_id=0, has_side_effects=True, vmem_limit_bytes=67043328),
+            collective_id=0, has_side_effects=True, vmem_limit_bytes=52 * 2**20),
         name="block",
-    )(queries, keys, values, norm_gain.reshape(1, D), expert_ids.reshape(1, T), w_in, w_out)
+    )(queries, keys, values, pltpu.with_memory_space_constraint(norm_gain, pltpu.HBM),
+      pltpu.with_memory_space_constraint(expert_ids.reshape(1, T), pltpu.HBM), w_in, w_out)
 
 
 def solution(mesh):

time: 91.3 us -> 79.1 us (0.87)
  Pallas kernels: 86.8 us -> 77.9 us
  local copies, waits for them, and re-layouts: 3.92 us -> 1.15 us
    pallas_call x1, Pallas kernels: 86.8 us -> 77.9 us  [shards(): pl.pallas_call(body, out_shape=jax.ShapeDtypeStruct((T, D), BF16), in_spe...]
    unnamed x1, local copies, waits for them, and re-layouts: 2.65 us -> 1.15 us
    reshape x1 -> x0, local copies, waits for them, and re-layouts: 1.27 us -> none  [shards(): norm_gain.reshape(1, D)]
where the time goes in v2:
time: 79.1 us; the launch traced here: 79 us
  Pallas kernels  77.9 us (98%)
  local copies, waits for them, and re-layouts  1.15 us (1%)
    pallas_call x1, Pallas kernels, shards(): pl.pallas_call(body, out_shape=jax.ShapeDtypeStruct((T, D), BF16), in_spe...  77.9 us

profile of v2, /device:TPU:0, one launch (start us, length us, event | category | flops | bytes accessed | tf_op | source)
XLA Modules:
  0.0 79.0 jit_solution(13463391143325776101)
XLA Ops:
  0.0 77.9 %block.1 = bf16[1024,768]{1,0:T(8,128)(2,1)S(1)} custom-call(bf16[1024,768]{1,0:T(8,128)(2,1)} %q_hbm.1, bf16[1024,768]{1,0:T(8,128)(2,1)} %k_hbm.1, bf16[1024,768]{1,0:T(8,128)(2,1)} %v_hbm.1, f32[768]{0:T(1024)} %gain_hbm.1, s32[1,1024]{1,0:T(1,128)} %bitcast.1, bf16[2,768,3072]{2,1,0:T(8,128)(2,1)} %win_hbm.1, bf16[2,3072,768]{2,1,0:T(8,128)(2,1)} %wout_hbm.1), custom_call_target="tpu_custom_call" | custom-call | tf_op jit(solution)/shard_map/block/pallas_call | solution.py:341
  77.9 1.1 %copy.9 = bf16[1024,768]{1,0:T(8,128)(2,1)} copy(bf16[1024,768]{1,0:T(8,128)(2,1)S(1)} %block.1) | data formatting | bytes 3145728

commit v3 on v2

--- a/solution.py
+++ b/solution.py
@@ -18,7 +18,7 @@
 PAIRS = 6
 C = 256
 NC = T // C
-OWN = 48
+OWN = 24
 CH = 3
 M = 512
 
@@ -27,8 +27,12 @@
     return sum((0, 1, 2, 1)[g] for g in (o // 16, o // 4 % 4, o % 4))
 
 
+SPLIT = 4
 ORDER = sorted(range(1, N), key=lambda o: (-hops(o), o * 37 % 64))
 MIXED = [o * 21 % 64 for o in range(1, N)]
+
+NEAR = [o for o in ORDER if hops(o) < 3]
+MIDWAY = [o for o in ORDER if hops(o) == 3]
 
 
 def dot(a, b):
@@ -67,6 +71,12 @@
     def other(o):
         return ys[o // 16] + zs[o // 4 % 4] + xs[o % 4]
 
+    mine = jnp.where(my < 2, me, ys[2] + zs[2] + xs[2])
+
+    def slice_of(o):
+        far = ys[(o // 16 + 2) % 4] + zs[(o // 4 + 2) % 4] + xs[(o + 2) % 4]
+        return jnp.where(other(o) < N // 2, other(o), far)
+
     def remote(src, dst, ssem, rsem, d):
         return pltpu.make_async_remote_copy(
             src_ref=src, dst_ref=dst, send_sem=ssem, recv_sem=rsem,
@@ -103,7 +113,7 @@
             vc = v_ref[c * C:(c + 1) * C, lanes(p)]
             total = total + jnp.where(diag, dot_tn(kc, vc), 0.0)
         compact = jnp.where(low, total[:64], total[64:])
-        st_send[pl.ds(p * 8, 8)] = compact.reshape(8, 8, 128).astype(BF16)
+        st_send[pl.ds(p * 4, 4)] = compact.reshape(4, 2, 8, 128).astype(BF16)
         return 0
     lax.fori_loop(0, PAIRS, states, 0)
 
@@ -129,15 +139,15 @@
 
     pl.semaphore_wait(barrier, N - 1)
     for o in ORDER:
-        d = other(o)
-
-        @pl.when(d < OWN)
-        def _(d=d):
-            remote(st_send.at[d], st_recv.at[me], st_sem.at[0], st_sem.at[1], d).start()
-
-    @pl.when(me < OWN)
-    def _():
-        pltpu.make_async_copy(st_send.at[me], st_recv.at[me], self_sem.at[0]).start()
+        part = slice_of(o)
+
+        @pl.when(part < OWN)
+        def _(part=part, d=other(o)):
+            remote(st_send.at[part], st_recv.at[me], st_sem.at[0], st_sem.at[1], d).start()
+
+    @pl.when(mine < OWN)
+    def _():
+        pltpu.make_async_copy(st_send.at[mine], st_recv.at[me], self_sem.at[0]).start()
 
     loads[4].wait()
     tri = lax.broadcasted_iota(jnp.int32, (C, C), 0) >= lax.broadcasted_iota(jnp.int32, (C, C), 1)
@@ -154,22 +164,30 @@
             mixed_ref[rows, lanes(p)] = (dot(s0, jnp.where(low, vc, zero)) + dot(s1, jnp.where(low, zero, vc))
                                          + dot(qc, kv_ref[p, c].astype(BF16)))
         return 0
-    lax.fori_loop(0, PAIRS, local, 0)
-
-    @pl.when(me < OWN)
-    def _():
-        pltpu.make_async_copy(st_send.at[me], st_recv.at[me], self_sem.at[0]).wait()
+    lax.fori_loop(0, SPLIT, local, 0)
+
+    @pl.when(mine < OWN)
+    def _():
+        pltpu.make_async_copy(st_send.at[mine], st_recv.at[me], self_sem.at[0]).wait()
         pltpu.make_async_copy(st_recv.at[pl.ds(0, N - 1)], st_recv.at[pl.ds(0, N - 1)], st_sem.at[1]).wait()
 
         def step(i, run):
             pre_send[i] = run.astype(BF16)
             return run + st_recv[i].astype(F32)
-        lax.fori_loop(0, N, step, jnp.zeros((8, 128), F32), unroll=8)
-
-        for o in ORDER:
+        lax.fori_loop(0, N, step, jnp.zeros((2, 8, 128), F32), unroll=8)
+
+        for o in NEAR:
             d = other(o)
-            remote(pre_send.at[d], pre_recv.at[me], pre_sem.at[0], pre_sem.at[1], d).start()
-        pltpu.make_async_copy(pre_send.at[me], pre_recv.at[me], self_sem.at[1]).start()
+            remote(pre_send.at[d], pre_recv.at[mine], pre_sem.at[0], pre_sem.at[1], d).start()
+
+        @pl.when(my < 2)
+        def _():
+            for o in MIDWAY:
+                d = other(o)
+                remote(pre_send.at[d], pre_recv.at[mine], pre_sem.at[0], pre_sem.at[1], d).start()
+        pltpu.make_async_copy(pre_send.at[me], pre_recv.at[mine], self_sem.at[1]).start()
+
+    lax.fori_loop(SPLIT, PAIRS, local, 0)
 
     def pick(ch):
         return jnp.where(lax.broadcasted_iota(jnp.int32, (M, T), 0) == slot_row - ch * M, 1.0, 0.0).astype(BF16)
@@ -182,30 +200,32 @@
         early_ref[:, cols] = dot(first_pick, high) + dot(first_pick, (m - high.astype(F32)).astype(BF16))
         earlyq_ref[:, cols] = dot(first_pick, q_ref[:, cols]).astype(BF16)
 
-    @pl.when(me < OWN)
-    def _():
-        pltpu.make_async_copy(pre_send.at[me], pre_recv.at[me], self_sem.at[1]).wait()
+    @pl.when(mine < OWN)
+    def _():
+        pltpu.make_async_copy(pre_send.at[me], pre_recv.at[mine], self_sem.at[1]).wait()
         pltpu.make_async_copy(pre_recv.at[pl.ds(0, OWN - 1)], pre_recv.at[pl.ds(0, OWN - 1)], pre_sem.at[1]).wait()
 
-    @pl.when(me >= OWN)
+    @pl.when(mine >= OWN)
     def _():
         pltpu.make_async_copy(pre_recv, pre_recv, pre_sem.at[1]).wait()
 
     for p in range(PAIRS):
-        compact = pre_recv[pl.ds(p * 8, 8)].astype(F32).reshape(64, 128)
+        compact = pre_recv[pl.ds(p * 4, 4)].astype(F32).reshape(64, 128)
         cst_ref[p, :64] = jnp.where(low, compact, 0.0).astype(BF16)
         cst_ref[p, 64:] = jnp.where(low, 0.0, compact).astype(BF16)
 
     gain = gain_ref[...].reshape(1, D)
 
-    def send_rows(ch):
-        for o in MIXED:
+    def send_rows(ch, offsets):
+        for o in offsets:
             d = other(o)
             remote(disp_send.at[ch, d], disp_recv.at[ch, me], disp_ssem.at[ch], disp_rsem.at[ch], d).start()
+
+    def keep_own(ch):
         pltpu.make_async_copy(disp_send.at[ch, me], disp_recv.at[ch, me], self_sem.at[2 + ch]).start()
 
-    def finish_early(c, _):
-        rows = pl.ds(pl.multiple_of(c * 128, 128), 128)
+    for g in (2, 1, 3, 0):
+        rows = pl.ds(pl.multiple_of(ys[g] * 8, 128), 128)
         square = jnp.zeros((128, 128), F32)
         ms = []
         for p in range(PAIRS):
@@ -216,10 +236,9 @@
         scale = lax.rsqrt(jnp.sum(square, axis=1, keepdims=True) * (1.0 / D) + EPS)
         for p in range(PAIRS):
             y = ms[p] * scale * gain[:, p * 128:(p + 1) * 128]
-            disp_send[0, pl.ds(c * 16, 16), p] = y.reshape(16, 8, 128).astype(BF16)
-        return 0
-    lax.fori_loop(0, M // 128, finish_early, 0)
-    send_rows(0)
+            disp_send[0, pl.ds(ys[g], 16), p] = y.reshape(16, 8, 128).astype(BF16)
+    send_rows(0, MIXED)
+    keep_own(0)
 
     def finish(c, _):
         rows = pl.ds(pl.multiple_of(c * C, C), C)
@@ -240,7 +259,8 @@
             y = dot(this_pick, normed_ref[:, n * 256:(n + 1) * 256])
             disp_send[ch, :, 2 * n] = y[:, :128].reshape(N, 8, 128).astype(BF16)
             disp_send[ch, :, 2 * n + 1] = y[:, 128:].reshape(N, 8, 128).astype(BF16)
-        send_rows(ch)
+        send_rows(ch, MIXED)
+        keep_own(ch)
 
     top = lax.broadcasted_iota(jnp.int32, (1, 8, 128), 1) < 4
 
@@ -295,16 +315,22 @@
                 odd = jnp.where(top, pltpu.roll(o0, 4, 1), o1)
                 ret_send[ch, :, j] = jnp.stack([even, odd], axis=1).reshape(N, 8, 128).astype(BF16)
 
-        for o in (MIXED if ch < 2 else ORDER):
-            d = other(o)
-            remote(ret_send.at[ch, d], ret_recv.at[ch, me], ret_ssem.at[ch], ret_rsem.at[ch], d).start()
+        for part in range(1 if ch < 2 else 2):
+            cols = pl.ds(0, 6) if ch < 2 else pl.ds(3 * part, 3)
+            for o in (MIXED if part == 0 else ORDER):
+                d = other(o)
+                remote(ret_send.at[ch, d, cols], ret_recv.at[ch, me, cols],
+                       ret_ssem.at[ch], ret_rsem.at[ch + part], d).start()
         pltpu.make_async_copy(ret_send.at[ch, me], ret_recv.at[ch, me], self_sem.at[5 + ch]).start()
 
-    for ch in range(CH):
+    def level(ch, js):
+        for j in js:
+            a_ref[:, j * 128:(j + 1) * 128] = ret_recv[ch, :, j].astype(F32).reshape(M, 128).astype(BF16)
+
+    for ch in range(2):
         pltpu.make_async_copy(ret_send.at[ch, me], ret_recv.at[ch, me], self_sem.at[5 + ch]).wait()
         bulk(ret_recv.at[ch], ret_rsem.at[ch]).wait()
-        for j in range(6):
-            a_ref[:, j * 128:(j + 1) * 128] = ret_recv[ch, :, j].astype(F32).reshape(M, 128).astype(BF16)
+        level(ch, range(6))
 
         def unpack(c, _):
             rows = pl.ds(pl.multiple_of(c * C, C), C)
@@ -314,21 +340,42 @@
                 y = dot(back, a_ref[:, cols])
                 if ch == 0:
                     acc_ref[rows, cols] = y
-                elif ch == 1:
+                else:
                     acc_ref[rows, cols] = normed_ref[rows, cols].astype(F32) + (acc_ref[rows, cols] + y)
-                else:
-                    out_ref[rows, cols] = (acc_ref[rows, cols] + y).astype(BF16)
             return 0
         lax.fori_loop(0, NC, unpack, 0)
 
-    @pl.when(me < OWN)
-    def _():
-        pltpu.make_async_copy(st_send.at[pl.ds(0, OWN - 1)], st_send.at[pl.ds(0, OWN - 1)], st_sem.at[0]).wait()
-        bulk(pre_send, pre_sem.at[0]).wait()
-
-    @pl.when(me >= OWN)
-    def _():
-        pltpu.make_async_copy(st_send, st_send, st_sem.at[0]).wait()
+    for c in range(NC):
+        h_ref[:C, c * M:(c + 1) * M] = spread(slot_ref[c * C:(c + 1) * C, :] - 2 * M)
+    pltpu.make_async_copy(ret_send.at[2, me], ret_recv.at[2, me], self_sem.at[7]).wait()
+    for part in range(2):
+        got = ret_recv.at[2, pl.ds(0, N - 1), pl.ds(3 * part, 3)]
+        pltpu.make_async_copy(got, got, ret_rsem.at[2 + part]).wait()
+        level(2, range(3 * part, 3 * part + 3))
+        for c in range(NC):
+            rows = slice(c * C, (c + 1) * C)
+            cols = slice(part * 384, (part + 1) * 384)
+            y = dot(h_ref[:C, c * M:(c + 1) * M], a_ref[:, cols])
+            out_ref[rows, cols] = (acc_ref[rows, cols] + y).astype(BF16)
+
+    def left(buf, count, sem):
+        pltpu.make_async_copy(buf.at[pl.ds(0, count)], buf.at[pl.ds(0, count)], sem).wait()
+
+    @pl.when(mine < OWN)
+    def _():
+        left(st_recv, 2 * OWN - 1, st_sem.at[0])
+
+        @pl.when(my < 2)
+        def _():
+            left(pre_send, len(NEAR) + len(MIDWAY), pre_sem.at[0])
+
+        @pl.when(my >= 2)
+        def _():
+            left(pre_send, len(NEAR), pre_sem.at[0])
+
+    @pl.when(mine >= OWN)
+    def _():
+        left(st_recv, 2 * OWN, st_sem.at[0])
     for ch in range(CH):
         bulk(disp_send.at[ch], disp_ssem.at[ch]).wait()
         bulk(ret_send.at[ch], ret_ssem.at[ch]).wait()
@@ -349,14 +396,14 @@
             pltpu.VMEM((2, D, FF), BF16), pltpu.VMEM((2, FF, D), BF16),
             pltpu.VMEM((PAIRS, NC, 128, 128), F32), pltpu.VMEM((PAIRS, 128, 128), BF16),
             pltpu.VMEM((T, D), F32), pltpu.VMEM((T, D), BF16),
-            pltpu.VMEM((OWN, 8, 128), BF16), pltpu.VMEM((N, 8, 128), BF16),
-            pltpu.VMEM((N, 8, 128), BF16), pltpu.VMEM((OWN, 8, 128), BF16),
+            pltpu.VMEM((OWN, 2, 8, 128), BF16), pltpu.VMEM((N, 2, 8, 128), BF16),
+            pltpu.VMEM((N, 2, 8, 128), BF16), pltpu.VMEM((OWN, 2, 8, 128), BF16),
             pltpu.VMEM((T, 128), jnp.int32), pltpu.VMEM((M, D), F32), pltpu.VMEM((M, D), BF16),
             pltpu.VMEM((CH, N, 6, 8, 128), BF16), pltpu.VMEM((CH, N, 6, 8, 128), BF16),
             pltpu.VMEM((CH, N, 6, 8, 128), BF16), pltpu.VMEM((CH, N, 6, 8, 128), BF16),
             pltpu.VMEM((M, D), BF16), pltpu.VMEM((M, FF), BF16), pltpu.VMEM((T, D), F32),
             dma((5,)), dma((4,)), dma((8,)), dma((2,)), dma((2,)),
-            dma((CH,)), dma((CH,)), dma((CH,)), dma((CH,)),
+            dma((CH,)), dma((CH,)), dma((CH,)), dma((CH + 1,)),
         ],
         compiler_params=pltpu.CompilerParams(
             collective_id=0, has_side_effects=True, vmem_limit_bytes=52 * 2**20),

time: 79.1 us -> 78.2 us (0.989)
  Pallas kernels: 77.9 us -> 76.4 us
    pallas_call x1, Pallas kernels: 77.9 us -> 76.4 us  [shards(): pl.pallas_call(body, out_shape=jax.ShapeDtypeStruct((T, D), BF16), in_spe...]
where the time goes in v3:
time: 78.2 us; the launch traced here: 77.6 us
  Pallas kernels  76.4 us (98%)
  local copies, waits for them, and re-layouts  1.15 us (1%)
    pallas_call x1, Pallas kernels, shards(): pl.pallas_call(body, out_shape=jax.ShapeDtypeStruct((T, D), BF16), in_spe...  76.4 us

profile of v3, /device:TPU:0, one launch (start us, length us, event | category | flops | bytes accessed | tf_op | source)
XLA Modules:
  0.0 77.6 jit_solution(11398994016994533905)
XLA Ops:
  0.0 76.4 %block.1 = bf16[1024,768]{1,0:T(8,128)(2,1)S(1)} custom-call(bf16[1024,768]{1,0:T(8,128)(2,1)} %q_hbm.1, bf16[1024,768]{1,0:T(8,128)(2,1)} %k_hbm.1, bf16[1024,768]{1,0:T(8,128)(2,1)} %v_hbm.1, f32[768]{0:T(1024)} %gain_hbm.1, s32[1,1024]{1,0:T(1,128)} %bitcast.1, bf16[2,768,3072]{2,1,0:T(8,128)(2,1)} %win_hbm.1, bf16[2,3072,768]{2,1,0:T(8,128)(2,1)} %wout_hbm.1), custom_call_target="tpu_custom_call" | custom-call | tf_op jit(solution)/shard_map/block/pallas_call | solution.py:388
  76.5 1.1 %copy.9 = bf16[1024,768]{1,0:T(8,128)(2,1)} copy(bf16[1024,768]{1,0:T(8,128)(2,1)S(1)} %block.1) | data formatting | bytes 3145728

commit v4 on v3

--- a/solution.py
+++ b/solution.py
@@ -93,8 +93,6 @@
         c.start()
     weights = [pltpu.make_async_copy(s.at[e], d.at[e], w_sem.at[2 * e + i])
                for e in range(2) for i, (s, d) in enumerate(((win_hbm, win), (wout_hbm, wout)))]
-    for c in weights:
-        c.start()
 
     lane = lax.broadcasted_iota(jnp.int32, (1, 128), 1)
     low = lane < 64
@@ -150,6 +148,8 @@
         pltpu.make_async_copy(st_send.at[mine], st_recv.at[me], self_sem.at[0]).start()
 
     loads[4].wait()
+    for c in weights:
+        c.start()
     tri = lax.broadcasted_iota(jnp.int32, (C, C), 0) >= lax.broadcasted_iota(jnp.int32, (C, C), 1)
 
     def local(p, _):
@@ -315,12 +315,24 @@
                 odd = jnp.where(top, pltpu.roll(o0, 4, 1), o1)
                 ret_send[ch, :, j] = jnp.stack([even, odd], axis=1).reshape(N, 8, 128).astype(BF16)
 
-        for part in range(1 if ch < 2 else 2):
-            cols = pl.ds(0, 6) if ch < 2 else pl.ds(3 * part, 3)
-            for o in (MIXED if part == 0 else ORDER):
+        def give(d, cols, sem):
+            remote(ret_send.at[ch, d, cols], ret_recv.at[ch, me, cols], ret_ssem.at[ch], ret_rsem.at[sem], d).start()
+
+        if ch < 2:
+            for o in MIXED:
+                give(other(o), pl.ds(0, 6), ch)
+        else:
+            for o in MIXED:
                 d = other(o)
-                remote(ret_send.at[ch, d, cols], ret_recv.at[ch, me, cols],
-                       ret_ssem.at[ch], ret_rsem.at[ch + part], d).start()
+                give(d, pl.ds(0, 3), ch)
+
+                @pl.when(jnp.logical_or(ys[o // 16] == 0, zs[o // 4 % 4] == 0))
+                def _(d=d):
+                    give(d, pl.ds(3, 3), ch + 1)
+            for o in ORDER:
+                @pl.when(jnp.logical_not(jnp.logical_or(ys[o // 16] == 0, zs[o // 4 % 4] == 0)))
+                def _(d=other(o)):
+                    give(d, pl.ds(3, 3), ch + 1)
         pltpu.make_async_copy(ret_send.at[ch, me], ret_recv.at[ch, me], self_sem.at[5 + ch]).start()
 
     def level(ch, js):

time: 78.2 us -> 77.8 us (level)
  no operation moved by 1% of the time
where the time goes in v4:
time: 77.8 us; the launch traced here: 77.5 us
  Pallas kernels  76.3 us (98%)
  local copies, waits for them, and re-layouts  1.15 us (1%)
    pallas_call x1, Pallas kernels, shards(): pl.pallas_call(body, out_shape=jax.ShapeDtypeStruct((T, D), BF16), in_spe...  76.3 us

profile of v4, /device:TPU:0, one launch (start us, length us, event | category | flops | bytes accessed | tf_op | source)
XLA Modules:
  0.0 77.5 jit_solution(17837339852007829447)
XLA Ops:
  0.0 76.3 %block.1 = bf16[1024,768]{1,0:T(8,128)(2,1)S(1)} custom-call(bf16[1024,768]{1,0:T(8,128)(2,1)} %q_hbm.1, bf16[1024,768]{1,0:T(8,128)(2,1)} %k_hbm.1, bf16[1024,768]{1,0:T(8,128)(2,1)} %v_hbm.1, f32[768]{0:T(1024)} %gain_hbm.1, s32[1,1024]{1,0:T(1,128)} %bitcast.1, bf16[2,768,3072]{2,1,0:T(8,128)(2,1)} %win_hbm.1, bf16[2,3072,768]{2,1,0:T(8,128)(2,1)} %wout_hbm.1), custom_call_target="tpu_custom_call" | custom-call | tf_op jit(solution)/shard_map/block/pallas_call | solution.py:400
  76.3 1.1 %copy.9 = bf16[1024,768]{1,0:T(8,128)(2,1)} copy(bf16[1024,768]{1,0:T(8,128)(2,1)S(1)} %block.1) | data formatting | bytes 3145728

commit v5 on v4

--- a/solution.py
+++ b/solution.py
@@ -64,9 +64,10 @@
          ld_sem, w_sem, self_sem, st_sem, pre_sem, disp_ssem, disp_rsem, ret_ssem, ret_rsem):
     me = lax.axis_index("seq")
     my, mz, mx = me // 16, lax.rem(me // 4, 4), lax.rem(me, 4)
-    ys = [lax.rem(my + g, 4) * 16 for g in range(4)]
-    zs = [lax.rem(mz + g, 4) * 4 for g in range(4)]
-    xs = [lax.rem(mx + g, 4) for g in range(4)]
+    turn = 1 + 2 * lax.axis_index("dp")
+    ys = [lax.rem(my + g * turn, 4) * 16 for g in range(4)]
+    zs = [lax.rem(mz + g * turn, 4) * 4 for g in range(4)]
+    xs = [lax.rem(mx + g * turn, 4) for g in range(4)]
 
     def other(o):
         return ys[o // 16] + zs[o // 4 % 4] + xs[o % 4]

time: 77.8 us -> 77.6 us (level)
  no operation moved by 1% of the time
where the time goes in v5:
time: 77.6 us; the launch traced here: 77.5 us
  Pallas kernels  76.4 us (98%)
  local copies, waits for them, and re-layouts  1.15 us (1%)
    pallas_call x1, Pallas kernels, shards(): pl.pallas_call(body, out_shape=jax.ShapeDtypeStruct((T, D), BF16), in_spe...  76.4 us

profile of v5, /device:TPU:0, one launch (start us, length us, event | category | flops | bytes accessed | tf_op | source)
XLA Modules:
  0.0 77.5 jit_solution(7773148859987820487)
XLA Ops:
  0.0 76.4 %block.1 = bf16[1024,768]{1,0:T(8,128)(2,1)S(1)} custom-call(bf16[1024,768]{1,0:T(8,128)(2,1)} %q_hbm.1, bf16[1024,768]{1,0:T(8,128)(2,1)} %k_hbm.1, bf16[1024,768]{1,0:T(8,128)(2,1)} %v_hbm.1, f32[768]{0:T(1024)} %gain_hbm.1, s32[1,1024]{1,0:T(1,128)} %bitcast.1, bf16[2,768,3072]{2,1,0:T(8,128)(2,1)} %win_hbm.1, bf16[2,3072,768]{2,1,0:T(8,128)(2,1)} %wout_hbm.1), custom_call_target="tpu_custom_call" | custom-call | tf_op jit(solution)/shard_map/block/pallas_call | solution.py:401
  76.4 1.1 %copy.9 = bf16[1024,768]{1,0:T(8,128)(2,1)} copy(bf16[1024,768]{1,0:T(8,128)(2,1)S(1)} %block.1) | data formatting | bytes 3145728
